TPU v7x, 256 devices: a whole 4x4x8 slice. The times are simulated.
256 devices in a mesh: outer: 32 (over z, x), inner: 8 (over y, core).
Axes of the slice: x: 4, y: 4, z: 8, core: 2. Of those that a mesh axis runs over, the one named last changes fastest.
Arguments:
- query: bfloat16 [32768, 32, 128], P(('outer', 'inner')), may hold values from -6 to 6
- keys: bfloat16 [32768, 32, 128], P(('outer', 'inner')), may hold values from -6 to 6
- value: bfloat16 [32768, 32, 128], P(('outer', 'inner')), may hold values from -6 to 6
- beta: bfloat16 [32768, 32], P(('outer', 'inner')), may hold values from 0 to 1, as said below
Outputs:
- mixed: bfloat16 [32768, 32, 128], P(('outer', 'inner'))
Inputs may be any that keep to these rules, and one draw needn't show every extreme that they name: `beta`: each gate lies strictly between 0 and 1.
All inputs are finite; a program needn't handle non-finite values.
Results may differ from a plain program's by a relative error of at most 0.001.
Values may be sent and summed in bfloat16 or wider, within the bound.
No kernel may reach another device: no remote copies, remote signals or barrier semaphores. Data moves between devices by JAX's collectives and lax.ppermute only.
A program may use at most 128 MiB of HBM per device.

v0:
```python
import jax
import jax.numpy as jnp
from jax import lax
from jax.sharding import PartitionSpec as P

SPAN = 128
HIGH = lax.Precision.HIGHEST


def prefix(x, axis, combine, identity):
    peers, index = (lax.axis_size(axis), lax.axis_index(axis))
    everything = jax.tree.map(lambda part: lax.all_gather(part, axis), x)
    start = jax.tree.map(
        lambda part, zero: jnp.broadcast_to(jnp.asarray(zero, part.dtype), part.shape), x, identity
    )

    def step(k, before):
        reached = k < index
        new = combine(before, jax.tree.map(lambda part: part[k], everything))
        return jax.tree.map(lambda a, b: jnp.where(reached, a, b), new, before)

    return lax.fori_loop(0, peers, step, start)


def unit_rows(block):
    return block * lax.rsqrt(jnp.sum(block * block, axis=-1, keepdims=True) + 1e-06)


def unit_lower_inverse(strict_part):
    size = strict_part.shape[0]
    inverse = jnp.eye(size, dtype=jnp.float32) - strict_part
    power = jnp.dot(strict_part, strict_part, precision=HIGH)
    for level in range((size - 1).bit_length() - 1):
        inverse = inverse + jnp.dot(inverse, power, precision=HIGH)
        power = jnp.dot(power, power, precision=HIGH)
    return inverse


def span_terms(query_block, keys_c, value_c, beta_c):
    width = keys_c.shape[1]
    query_block = query_block.astype(jnp.float32)
    keys_c = keys_c.astype(jnp.float32)
    value_c = value_c.astype(jnp.float32)
    beta_c = beta_c.astype(jnp.float32)
    qnorm = unit_rows(query_block)
    knorm = unit_rows(keys_c)
    kbeta = knorm * beta_c[:, None]
    vbeta = value_c * beta_c[:, None]
    gram = jnp.dot(kbeta, knorm.T, precision=HIGH)
    inverse = unit_lower_inverse(jnp.tril(gram, -1))
    solved = jnp.dot(inverse, jnp.concatenate([kbeta, vbeta], axis=1), precision=HIGH)
    weights = solved[:, :width]
    updates = solved[:, width:]
    scores = jnp.tril(jnp.dot(qnorm, knorm.T, precision=HIGH))
    return (qnorm, knorm, weights, updates, scores)


def combine_pairs(earlier, later):
    trans_a, offset_a = earlier
    trans_b, offset_b = later
    merged = jnp.einsum("hij,hjk->hik", trans_b, trans_a, precision=HIGH)
    shifted = jnp.einsum("hij,hjk->hik", trans_b, offset_a, precision=HIGH) + offset_b
    return (merged, shifted)


def shards(query, keys, value, beta):
    qhead, khead, vhead, bhead = (
        lax.all_to_all(query, "inner", split_axis=1, concat_axis=0, tiled=True),
        lax.all_to_all(keys, "inner", split_axis=1, concat_axis=0, tiled=True),
        lax.all_to_all(value, "inner", split_axis=1, concat_axis=0, tiled=True),
        lax.all_to_all(beta, "inner", split_axis=1, concat_axis=0, tiled=True),
    )
    length, groups, width = qhead.shape
    count = length // SPAN

    def blocks(array):
        return jnp.transpose(array.reshape(count, SPAN, groups, width), (0, 2, 1, 3))

    bblk = jnp.transpose(bhead.reshape(count, SPAN, groups), (0, 2, 1))
    terms_fn = jax.vmap(jax.vmap(span_terms))
    qnorm, knorm, weights, updates, scores = terms_fn(
        blocks(qhead), blocks(khead), blocks(vhead), bblk
    )
    eye = jnp.broadcast_to(jnp.eye(width, dtype=jnp.float32), (groups, width, width))
    zeros = jnp.zeros((groups, width, width), jnp.float32)
    joined_parts = jnp.concatenate([eye, zeros], axis=2)

    def pair_step(carried, kpart, wpart, upart):
        product = jnp.einsum("hcd,hde->hce", wpart, carried, precision=HIGH)
        change = jnp.concatenate([-product[..., :width], upart - product[..., width:]], axis=2)
        nextpair = carried + jnp.einsum("hcd,hce->hde", kpart, change, precision=HIGH)
        return (nextpair, change)

    def transition_only(carried, inputs):
        kpart, wpart, upart = inputs
        nextpair, change = pair_step(carried, kpart, wpart, upart)
        return (nextpair, None)

    final_pair, _ = lax.scan(transition_only, joined_parts, (knorm, weights, updates))
    block_trans = final_pair[..., :width]
    block_offset = final_pair[..., width:]
    _, incoming = prefix((block_trans, block_offset), "outer", combine_pairs, (eye, zeros))

    def advance(state, inputs):
        qpart, kpart, wpart, upart, spart = inputs
        delta = upart - jnp.einsum("hcd,hde->hce", wpart, state, precision=HIGH)
        result = jnp.einsum("hcd,hde->hce", qpart, state, precision=HIGH) + jnp.einsum(
            "hcs,hse->hce", spart, delta, precision=HIGH
        )
        state = state + jnp.einsum("hcd,hce->hde", kpart, delta, precision=HIGH)
        return (state, result.astype(jnp.bfloat16))

    _, outputs = lax.scan(advance, incoming, (qnorm, knorm, weights, updates, scores))
    token_major = jnp.transpose(outputs, (0, 2, 1, 3)).reshape(length, groups, width)
    return lax.all_to_all(token_major, "inner", split_axis=0, concat_axis=1, tiled=True)


def solution(mesh):
    placed = (
        P(("outer", "inner"), None, None),
        P(("outer", "inner"), None, None),
        P(("outer", "inner"), None, None),
        P(("outer", "inner"), None),
    )
    return jax.shard_map(
        shards,
        mesh=mesh,
        in_specs=placed,
        out_specs=P(("outer", "inner"), None, None),
        check_vma=False,
    )
```

profile of v0, /device:TPU:1, one launch (start us, length us, event | category | flops | bytes accessed | tf_op | source)
XLA Modules:
  0.0 445.4 jit_solution(17959281910144616222)
XLA Ops:
  6.5 6.5 %all-to-all-start.1 = ((bf16[128,8,4]{0,2,1:T(4,128)(2,1)}), bf16[128,8,4]{0,2,1:T(4,128)(2,1)S(1)}, u32[]{:S(2)}, u32[]{:S(2)}) async-start(bf16[128,8,4]{0,2,1:T(4,128)(2,1)} %bitcast.145), calls=%async_computation.1 | async-start | bytes 16384 | tf_op jit(solution)/shard_map/all_to_all | solution.py:71
  13.0 2.7 copy.24
  15.7 1.9 all-to-all-done.1
  17.6 4.2 all-to-all-start
  23.4 13.5 %all-to-all-done = bf16[128,32,128]{2,0,1:T(8,128)(2,1)S(1)} async-done(((bf16[128,32,128]{2,0,1:T(8,128)(2,1)}), bf16[128,32,128]{2,0,1:T(8,128)(2,1)S(1)}, u32[]{:S(2)}, u32[]{:S(2)}) %all-to-all-start) | async-done | bytes 1048608 | tf_op jit(solution)/shard_map/all_to_all | solution.py:69
  36.9 4.3 all-to-all-start.2
  41.9 6.5 %fusion.57 = f32[8,4,128,128]{3,2,1,0:T(8,128)S(1)} fusion(bf16[128,8,4,128]{3,0,2,1:T(8,128)(2,1)S(1)} %bitcast.135, f32[8,4,128]{2,1,0:T(4,128)S(1)} %add_rsqrt_fusion.1, f32[8,4,128]{2,1,0:T(4,128)S(1)} %convert_bitcast_fusion.3), kind=kOutput, calls=%fused_computation.68 | convolution fusion | flops 807927808 | bytes 3178496 | tf_op jit(solution)/shard_map/vmap(vmap())/dot_general | solution.py:49
  48.4 2.2 fusion.51
  50.6 2.5 subtract_add_fusion
  53.0 2.0 fusion.75
  55.1 2.0 fusion.77
  57.1 2.2 fusion.76
  59.3 2.2 fusion.78
  61.5 2.3 convolution_add_fusion.5
  63.8 2.0 fusion.80
  65.8 2.2 fusion.79
  68.0 2.0 fusion.81
  70.1 2.5 convolution_add_fusion.4
  73.9 3.5 fusion.82
  77.4 2.2 fusion.59
  80.4 4.3 fusion.35
  84.7 2.6 fusion.73
  87.3 2.9 copy.26
  90.2 33.9 %while.36 = (s32[]{:T(128)}, f32[4,128,256]{2,1,0:T(8,128)S(1)}, f32[8,4,128,128]{2,3,1,0:T(8,128)}, f32[8,4,128,128]{3,2,1,0:T(8,128)}, f32[8,4,128,128]{3,2,1,0:T(8,128)}, /*index=5*/s32[]{:T(128)}) while((s32[]{:T(128)}, f32[4,128,256]{2,1,0:T(8,128)S(1)}, f32[8,4,128,128]{2,3,1,0:T(8,128)}, f32[8,4,128,128]{3,2,1,0:T(8,128)}, ...), condition=%wide.region_2.3_spmd, body=%wide.region_1.0_spmd.sunk | while | flops 403046400 | bytes 4457545 | solution.py:99
  90.2 1.5 fusion.129
  92.8 1.7 convolution_add_fusion.8
  94.4 1.5 fusion.129
  97.0 1.7 convolution_add_fusion.8
  98.7 1.5 fusion.129
  101.2 1.7 convolution_add_fusion.8
  102.9 1.5 fusion.129
  105.5 1.7 convolution_add_fusion.8
  107.2 1.5 fusion.129
  109.7 1.7 convolution_add_fusion.8
  111.4 1.5 fusion.129
  114.0 1.7 convolution_add_fusion.8
  115.7 1.5 fusion.129
  118.2 1.7 convolution_add_fusion.8
  119.9 1.5 fusion.129
  122.5 1.7 convolution_add_fusion.8
  127.2 5.1 %all-to-all-start.3 = ((bf16[128,32,128]{2,0,1:T(8,128)(2,1)}), bf16[128,32,128]{2,0,1:T(8,128)(2,1)S(1)}, u32[]{:S(2)}, u32[]{:S(2)}) async-start(bf16[128,32,128]{2,0,1:T(8,128)(2,1)} %copy.27), calls=%async_computation.3 | async-start | bytes 2097152 | tf_op jit(solution)/shard_map/all_to_all | solution.py:68
  132.3 15.0 %all-to-all-done.3 = bf16[128,32,128]{2,0,1:T(8,128)(2,1)S(1)} async-done(((bf16[128,32,128]{2,0,1:T(8,128)(2,1)}), bf16[128,32,128]{2,0,1:T(8,128)(2,1)S(1)}, u32[]{:S(2)}, u32[]{:S(2)}) %all-to-all-start.3) | async-done | bytes 1048608 | tf_op jit(solution)/shard_map/all_to_all | solution.py:68
  148.0 2.0 fusion.40
  149.9 6.2 %convolution_select_fusion = f32[8,4,128,128]{3,2,1,0:T(8,128)} fusion(bf16[128,8,4,128]{3,0,2,1:T(8,128)(2,1)S(1)} %bitcast.136, f32[8,4,128]{2,1,0:T(4,128)S(1)} %add_rsqrt_fusion.1, pred[128,128]{1,0:T(8,128)(4,1)S(1)} %iota_compare_fusion, bf16[128,8,4,128]{3,0,2,1:T(8,128)(2,1)S(1)} %bitcast.138, f32[8,4,128]{2,1,0:T(4,128)S(1)} %add_rsqrt_fusion), kind=kOutput, calls=%fused_computation.67 | convolution fusion | flops 807927808 | bytes 4243456 | tf_op jit(solution)/shard_map/vmap(vmap())/dot_general | solution.py:54
  156.1 69.1 %all-gather.5.cloned.1.call-done = f32[128,128,128]{2,1,0:T(8,128)} async-done(((f32[4,128,128]{2,1,0:T(8,128)}), f32[128,128,128]{2,1,0:T(8,128)}) %all-gather.5.cloned.1.call-update) | async-done | bytes 8388624 | tf_op jit(solution)/shard_map/all_gather | solution.py:12
  225.2 98.0 %all-gather.7.cloned.1.call-done = f32[128,128,128]{2,1,0:T(8,128)} async-done(((f32[4,128,128]{2,1,0:T(8,128)}), f32[128,128,128]{2,1,0:T(8,128)}) %all-gather.7.cloned.1.call-update) | async-done | bytes 8388624 | tf_op jit(solution)/shard_map/all_gather | solution.py:12
  323.2 47.4 %while.38 = (s32[]{:T(128)}, f32[4,128,128]{2,1,0:T(8,128)S(1)}, s32[]{:T(128)}, f32[32,4,128,128]{3,2,1,0:T(8,128)}, f32[32,4,128,128]{3,2,1,0:T(8,128)}, /*index=5*/s32[]{:T(128)}, s32[]{:T(128)}) while((s32[]{:T(128)}, f32[4,128,128]{2,1,0:T(8,128)S(1)}, s32[]{:T(128)}, f32[32,4,128,128]{3,2,1,0:T(8,128)}, ...), condition=%wide.region_4.5_spmd.clone, body=%wide.region_3.4_spmd.clone.sunk | while | flops 100925440 | bytes 1837663 | solution.py:22
  326.2 1.4 fusion.142
  329.2 1.4 fusion.142
  332.2 1.4 fusion.142
  333.6 1.4 fusion.142
  336.6 1.4 fusion.142
  338.1 1.4 fusion.142
  341.1 1.4 fusion.142
  344.0 1.4 fusion.142
  348.5 1.4 fusion.142
  351.4 1.4 fusion.142
  354.4 1.4 fusion.142
  355.9 1.4 fusion.142
  358.9 1.4 fusion.142
  360.3 1.4 fusion.142
  370.7 44.7 %while.37 = (s32[]{:T(128)}, f32[4,128,128]{2,1,0:T(8,128)S(1)}, bf16[8,4,128,128]{3,2,0,1:T(8,128)(2,1)S(1)}, f32[8,4,128,128]{2,3,1,0:T(8,128)}, f32[8,4,128,1...) while((s32[]{:T(128)}, f32[4,128,128]{2,1,0:T(8,128)S(1)}, ...), condition=%wide.region_7.8_spmd, body=%wide.region_6.7_spmd.sunk | while | flops 402915328 | bytes 3804253 | solution.py:113
  416.2 20.2 %all_to_all.58 = bf16[1024,4,128]{2,1,0:T(4,128)(2,1)S(1)} all-to-all(bf16[1024,4,128]{2,1,0:T(4,128)(2,1)S(1)} %copy.30), channel_id=1, replica_groups=mesh['outer'=32,'inner'=8] {'inner'}, dimensions={0} | all-to-all | bytes 2097152 | tf_op jit(solution)/shard_map/all_to_all | solution.py:115
  436.6 1.6 copy.33
  (123 shorter events, 87.7 us)
Async XLA Ops:
  6.5 11.1 %all-to-all-start.1 = ((bf16[128,8,4]{0,2,1:T(4,128)(2,1)}), bf16[128,8,4]{0,2,1:T(4,128)(2,1)S(1)}, u32[]{:S(2)}, u32[]{:S(2)}) async-start(bf16[128,8,4]{0,2,1:T(4,128)(2,1)} %bitcast.145), calls=%async_computation.1 | async-start | bytes 16384 | tf_op jit(solution)/shard_map/all_to_all | solution.py:71
  13.0 8.8 %copy-start.3 = (bf16[128,32,128]{2,1,0:T(8,128)(2,1)S(1)}, bf16[128,32,128]{2,1,0:T(8,128)(2,1)}, u32[]{:S(2)}) copy-start(bf16[128,32,128]{2,1,0:T(8,128)(2,1)} %param.12) | copy-start | bytes 3145732
  17.6 19.3 %all-to-all-start = ((bf16[128,32,128]{2,0,1:T(8,128)(2,1)}), bf16[128,32,128]{2,0,1:T(8,128)(2,1)S(1)}, u32[]{:S(2)}, u32[]{:S(2)}) async-start(bf16[128,32,128]{2,0,1:T(8,128)(2,1)} %copy.24), calls=%async_computation | async-start | bytes 2097152 | tf_op jit(solution)/shard_map/all_to_all | solution.py:69
  36.9 40.5 %all-to-all-start.2 = ((bf16[128,32,128]{2,0,1:T(8,128)(2,1)}), bf16[128,32,128]{2,0,1:T(8,128)(2,1)S(1)}, u32[]{:S(2)}, u32[]{:S(2)}) async-start(bf16[128,32,128]{2,0,1:T(8,128)(2,1)} %copy.25), calls=%async_computation.2 | async-start | bytes 2097152 | tf_op jit(solution)/shard_map/all_to_all | solution.py:70
  41.3 184.0 %all-gather.5.cloned.1.call-start = ((), (), s32[]{:S(2)}) async-start(), calls=%async_computation.5 | async-start | bytes 8650752 | tf_op jit(solution)/shard_map/all_gather | solution.py:12
  72.6 1.3 copy-start
  77.4 2.2 copy-start.1
  77.4 3.0 copy-start.2
  124.1 1.6 copy-start.4
  125.0 198.2 %all-gather.7.cloned.1.call-start = ((), (), s32[]{:S(2)}) async-start(), calls=%async_computation.6 | async-start | bytes 8650752 | tf_op jit(solution)/shard_map/all_gather | solution.py:12
  127.2 20.2 %all-to-all-start.3 = ((bf16[128,32,128]{2,0,1:T(8,128)(2,1)}), bf16[128,32,128]{2,0,1:T(8,128)(2,1)S(1)}, u32[]{:S(2)}, u32[]{:S(2)}) async-start(bf16[128,32,128]{2,0,1:T(8,128)(2,1)} %copy.27), calls=%async_computation.3 | async-start | bytes 2097152 | tf_op jit(solution)/shard_map/all_to_all | solution.py:68
Sparse Core Ops, SparseCore 0:
  125.1 100.0 all-gather.4
  227.8 95.4 all-gather.6
where the time goes:
time: 451 us; the launch traced here: 445 us
  waiting for transfers between devices  198 us (44%)
  matrix products  160 us (35%)
  blocking collectives  20.2 us (4%)
  starting transfers between devices  20.1 us (4%)
  local copies, waits for them, and re-layouts  17.2 us (4%)
  between operations  13.9 us (3%)
  other arithmetic  13.7 us (3%)
    all_gather x2, waiting for transfers between devices, prefix(): everything = jax.tree.map(lambda part: lax.all_gather(part, axis), x)  167 us
    dot_general x32, matrix products, combine_pairs(): jnp.einsum('hij,hjk->hik', trans_b, offset_a, precision=HIGH) + offset_b  45.6 us
    all_to_all x1, blocking collectives, shards(): lax.all_to_all(token_major, 'inner', split_axis=0, concat_axis=1, tiled=T...  20.2 us
    dot_general x6, matrix products, unit_lower_inverse(): inverse = inverse + jnp.dot(inverse, power, precision=HIGH)  15.1 us
    all_to_all x1, waiting for transfers between devices, shards(): lax.all_to_all(query, 'inner', split_axis=1, concat_axis=0, tiled=True)  15 us
    all_to_all x1, waiting for transfers between devices, shards(): lax.all_to_all(keys, 'inner', split_axis=1, concat_axis=0, tiled=True)  13.5 us
    dot_general x8, matrix products, pair_step(): jnp.einsum('hcd,hce->hde', kpart, change, precision=HIGH)  13.3 us
    dot_general x8, matrix products, pair_step(): product = jnp.einsum('hcd,hde->hce', wpart, carried, precision=HIGH)  12.3 us
  transfers between devices with their start and end apart: 6, of which 5 were waited for; matrix products, arithmetic and copies ran while one was open for 11% of the time, Pallas kernels for 0%

commit v1 on v0

--- a/solution.py
+++ b/solution.py
@@ -1,3 +1,4 @@
+import functools
 import jax
 import jax.numpy as jnp
 from jax import lax
@@ -5,6 +6,21 @@
 
 SPAN = 128
 HIGH = lax.Precision.HIGHEST
+
+
+def views_bind(x_part, comm_axis):
+    return jnp.concatenate(
+        lax.all_to_all(
+            jnp.stack(jnp.split(x_part, lax.axis_size(comm_axis), 1), axis=0),
+            comm_axis,
+            split_axis=0,
+            concat_axis=0,
+        ),
+        0,
+    )
+
+
+fix_hubs = functools.partial(views_bind, comm_axis="inner")
 
 
 def prefix(x, axis, combine, identity):
@@ -65,7 +81,7 @@
 
 def shards(query, keys, value, beta):
     qhead, khead, vhead, bhead = (
-        lax.all_to_all(query, "inner", split_axis=1, concat_axis=0, tiled=True),
+        fix_hubs(query),
         lax.all_to_all(keys, "inner", split_axis=1, concat_axis=0, tiled=True),
         lax.all_to_all(value, "inner", split_axis=1, concat_axis=0, tiled=True),
         lax.all_to_all(beta, "inner", split_axis=1, concat_axis=0, tiled=True),

time: 451 us -> 451 us (level)
    unnamed x13 -> x19, local copies, waits for them, and re-layouts: 7.54 us -> 10.9 us
  transfers between devices with their start and end apart: 6 -> 6, of which waited for: 5 -> 5; matrix products, arithmetic and copies ran while one was open for 11% -> 12% of each run, Pallas kernels for 0% -> 0%
where the time goes in v1:
time: 451 us; the launch traced here: 445 us
  waiting for transfers between devices  194 us (43%)
  matrix products  160 us (35%)
  local copies, waits for them, and re-layouts  21.6 us (5%)
  blocking collectives  20.2 us (4%)
  starting transfers between devices  20.1 us (4%)
  between operations  13.9 us (3%)
  other arithmetic  13.7 us (3%)
    all_gather x2, waiting for transfers between devices, prefix(): everything = jax.tree.map(lambda part: lax.all_gather(part, axis), x)  163 us
    dot_general x32, matrix products, combine_pairs(): jnp.einsum('hij,hjk->hik', trans_b, offset_a, precision=HIGH) + offset_b  45.6 us
    all_to_all x1, blocking collectives, shards(): lax.all_to_all(token_major, 'inner', split_axis=0, concat_axis=1, tiled=T...  20.2 us
    dot_general x6, matrix products, unit_lower_inverse(): inverse = inverse + jnp.dot(inverse, power, precision=HIGH)  15.1 us
    all_to_all x1, waiting for transfers between devices, views_bind(): lax.all_to_all(jnp.stack(jnp.split(x_part, lax.axis_size(comm_axis), 1),...  15 us
    all_to_all x1, waiting for transfers between devices, shards(): lax.all_to_all(keys, 'inner', split_axis=1, concat_axis=0, tiled=True)  13.5 us
    dot_general x8, matrix products, pair_step(): jnp.einsum('hcd,hce->hde', kpart, change, precision=HIGH)  13.3 us
    dot_general x8, matrix products, pair_step(): product = jnp.einsum('hcd,hde->hce', wpart, carried, precision=HIGH)  12.3 us
  transfers between devices with their start and end apart: 6, of which 5 were waited for; matrix products, arithmetic and copies ran while one was open for 12% of the time, Pallas kernels for 0%

profile of v1, /device:TPU:1, one launch (start us, length us, event | category | flops | bytes accessed | tf_op | source)
XLA Modules:
  0.0 445.4 jit_solution(16557918071611647649)
XLA Ops:
  6.5 6.5 %all-to-all-start.1 = ((bf16[128,8,4]{0,2,1:T(4,128)(2,1)}), bf16[128,8,4]{0,2,1:T(4,128)(2,1)S(1)}, u32[]{:S(2)}, u32[]{:S(2)}) async-start(bf16[128,8,4]{0,2,1:T(4,128)(2,1)} %bitcast.169), calls=%async_computation.1 | async-start | bytes 16384 | tf_op jit(solution)/shard_map/all_to_all | solution.py:87
  13.0 2.7 copy.45
  15.7 1.9 all-to-all-done.1
  17.6 4.2 all-to-all-start
  23.4 13.5 %all-to-all-done = bf16[128,32,128]{2,0,1:T(8,128)(2,1)S(1)} async-done(((bf16[128,32,128]{2,0,1:T(8,128)(2,1)}), bf16[128,32,128]{2,0,1:T(8,128)(2,1)S(1)}, u32[]{:S(2)}, u32[]{:S(2)}) %all-to-all-start) | async-done | bytes 1048608 | tf_op jit(solution)/shard_map/all_to_all | solution.py:85
  36.9 4.3 all-to-all-start.2
  41.9 6.5 %fusion.55 = f32[8,4,128,128]{3,2,1,0:T(8,128)S(1)} fusion(bf16[128,8,4,128]{3,0,2,1:T(8,128)(2,1)S(1)} %bitcast.161, f32[8,4,128]{2,1,0:T(4,128)S(1)} %add_rsqrt_fusion.1, f32[8,4,128]{2,1,0:T(4,128)S(1)} %convert_bitcast_fusion.2), kind=kOutput, calls=%fused_computation.67 | convolution fusion | flops 807927808 | bytes 3178496 | tf_op jit(solution)/shard_map/vmap(vmap())/dot_general | solution.py:65
  48.4 2.2 fusion.49
  50.6 2.5 subtract_add_fusion
  53.0 2.0 fusion.81
  55.1 2.0 fusion.83
  57.1 2.2 fusion.82
  59.3 2.2 fusion.84
  61.5 2.3 convolution_add_fusion.5
  63.8 2.0 fusion.86
  65.8 2.2 fusion.85
  68.0 2.0 fusion.87
  70.1 2.5 convolution_add_fusion.4
  73.9 3.5 fusion.88
  77.4 2.2 fusion.57
  80.4 4.3 fusion.35
  84.7 2.6 fusion.78
  87.3 2.9 copy.47
  90.2 33.9 %while.36 = (s32[]{:T(128)}, f32[4,128,256]{2,1,0:T(8,128)S(1)}, f32[8,4,128,128]{2,3,1,0:T(8,128)}, f32[8,4,128,128]{3,2,1,0:T(8,128)}, f32[8,4,128,128]{3,2,1,0:T(8,128)}, /*index=5*/s32[]{:T(128)}) while((s32[]{:T(128)}, f32[4,128,256]{2,1,0:T(8,128)S(1)}, f32[8,4,128,128]{2,3,1,0:T(8,128)}, f32[8,4,128,128]{3,2,1,0:T(8,128)}, ...), condition=%wide.region_2.3_spmd, body=%wide.region_1.0_spmd.sunk | while | flops 403046400 | bytes 4457545 | solution.py:115
  90.2 1.5 fusion.135
  92.7 1.7 convolution_add_fusion.8
  94.4 1.5 fusion.135
  97.0 1.7 convolution_add_fusion.8
  98.7 1.5 fusion.135
  101.2 1.7 convolution_add_fusion.8
  102.9 1.5 fusion.135
  105.5 1.7 convolution_add_fusion.8
  107.1 1.5 fusion.135
  109.7 1.7 convolution_add_fusion.8
  111.4 1.5 fusion.135
  114.0 1.7 convolution_add_fusion.8
  115.6 1.5 fusion.135
  118.2 1.7 convolution_add_fusion.8
  119.9 1.5 fusion.135
  122.4 1.7 convolution_add_fusion.8
  131.6 5.1 %all-to-all-start.3 = ((bf16[8,128,4,128]{3,1,2,0:T(8,128)(2,1)}), bf16[8,128,4,128]{3,1,2,0:T(8,128)(2,1)S(1)}, u32[]{:S(2)}, u32[]{:S(2)}) async-start(bf16[8,128,4,128]{3,1,2,0:T(8,128)(2,1)} %fusion.66), calls=%async_computation.3 | async-start | bytes 2097152 | tf_op jit(solution)/shard_map/all_to_all | solution.py:13
  136.7 15.0 %all-to-all-done.3 = bf16[8,128,4,128]{3,1,2,0:T(8,128)(2,1)S(1)} async-done(((bf16[8,128,4,128]{3,1,2,0:T(8,128)(2,1)}), bf16[8,128,4,128]{3,1,2,0:T(8,128)(2,1)S(1)}, u32[]{:S(2)}, u32[]{:S(2)}) %all-to-all-start.3) | async-done | bytes 1048608 | tf_op jit(solution)/shard_map/all_to_all | solution.py:13
  152.4 2.0 bitcast_multiply_fusion
  154.3 6.2 %convolution_select_fusion = f32[8,4,128,128]{3,2,1,0:T(8,128)} fusion(bf16[128,8,4,128]{3,0,2,1:T(8,128)(2,1)S(1)} %bitcast.162, f32[8,4,128]{2,1,0:T(4,128)S(1)} %add_rsqrt_fusion.1, pred[128,128]{1,0:T(8,128)(4,1)S(1)} %iota_compare_fusion, bf16[8,128,4,128]{3,1,2,0:T(8,128)(2,1)S(1)} %all-to-all-done.3, f32[8,4,128]{2,1,0:T(4,128)S(1)} %add_rsqrt_fusion), kind=kOutput, calls=%fused_computation.66 | convolution fusion | flops 807927808 | bytes 4243456 | tf_op jit(solution)/shard_map/vmap(vmap())/dot_general | solution.py:70
  160.6 64.6 %all-gather.5.cloned.1.call-done = f32[128,128,128]{2,1,0:T(8,128)} async-done(((f32[4,128,128]{2,1,0:T(8,128)}), f32[128,128,128]{2,1,0:T(8,128)}) %all-gather.5.cloned.1.call-update) | async-done | bytes 8388624 | tf_op jit(solution)/shard_map/all_gather | solution.py:28
  225.2 98.0 %all-gather.7.cloned.1.call-done = f32[128,128,128]{2,1,0:T(8,128)} async-done(((f32[4,128,128]{2,1,0:T(8,128)}), f32[128,128,128]{2,1,0:T(8,128)}) %all-gather.7.cloned.1.call-update) | async-done | bytes 8388624 | tf_op jit(solution)/shard_map/all_gather | solution.py:28
  323.2 47.4 %while.38 = (s32[]{:T(128)}, f32[4,128,128]{2,1,0:T(8,128)S(1)}, s32[]{:T(128)}, f32[32,4,128,128]{3,2,1,0:T(8,128)}, f32[32,4,128,128]{3,2,1,0:T(8,128)}, /*index=5*/s32[]{:T(128)}, s32[]{:T(128)}) while((s32[]{:T(128)}, f32[4,128,128]{2,1,0:T(8,128)S(1)}, s32[]{:T(128)}, f32[32,4,128,128]{3,2,1,0:T(8,128)}, ...), condition=%wide.region_4.5_spmd.clone, body=%wide.region_3.4_spmd.clone.sunk | while | flops 100925440 | bytes 1837663 | solution.py:38
  324.7 1.4 fusion.148
  326.2 1.4 fusion.148
  329.2 1.4 fusion.148
  332.1 1.4 fusion.148
  336.6 1.4 fusion.148
  339.5 1.4 fusion.148
  342.5 1.4 fusion.148
  344.0 1.4 fusion.148
  347.0 1.4 fusion.148
  348.4 1.4 fusion.148
  351.4 1.4 fusion.148
  354.4 1.4 fusion.148
  358.8 1.4 fusion.148
  364.8 1.4 fusion.148
  370.6 44.7 %while.37 = (s32[]{:T(128)}, f32[4,128,128]{2,1,0:T(8,128)S(1)}, bf16[8,4,128,128]{3,2,0,1:T(8,128)(2,1)S(1)}, f32[8,4,128,128]{2,3,1,0:T(8,128)}, f32[8,4,128,1...) while((s32[]{:T(128)}, f32[4,128,128]{2,1,0:T(8,128)S(1)}, ...), condition=%wide.region_7.8_spmd, body=%wide.region_6.7_spmd.sunk | while | flops 402915328 | bytes 3804253 | solution.py:129
  416.2 20.2 %all_to_all.54 = bf16[1024,4,128]{2,1,0:T(4,128)(2,1)S(1)} all-to-all(bf16[1024,4,128]{2,1,0:T(4,128)(2,1)S(1)} %copy.58), channel_id=1, replica_groups=mesh['outer'=32,'inner'=8] {'inner'}, dimensions={0} | all-to-all | bytes 2097152 | tf_op jit(solution)/shard_map/all_to_all | solution.py:131
  436.6 1.6 copy.61
  (131 shorter events, 92.1 us)
Async XLA Ops:
  6.5 11.1 %all-to-all-start.1 = ((bf16[128,8,4]{0,2,1:T(4,128)(2,1)}), bf16[128,8,4]{0,2,1:T(4,128)(2,1)S(1)}, u32[]{:S(2)}, u32[]{:S(2)}) async-start(bf16[128,8,4]{0,2,1:T(4,128)(2,1)} %bitcast.169), calls=%async_computation.1 | async-start | bytes 16384 | tf_op jit(solution)/shard_map/all_to_all | solution.py:87
  13.0 8.8 %copy-start.3 = (bf16[128,32,128]{2,1,0:T(8,128)(2,1)S(1)}, bf16[128,32,128]{2,1,0:T(8,128)(2,1)}, u32[]{:S(2)}) copy-start(bf16[128,32,128]{2,1,0:T(8,128)(2,1)} %param.12) | copy-start | bytes 3145732
  17.6 19.3 %all-to-all-start = ((bf16[128,32,128]{2,0,1:T(8,128)(2,1)}), bf16[128,32,128]{2,0,1:T(8,128)(2,1)S(1)}, u32[]{:S(2)}, u32[]{:S(2)}) async-start(bf16[128,32,128]{2,0,1:T(8,128)(2,1)} %copy.45), calls=%async_computation | async-start | bytes 2097152 | tf_op jit(solution)/shard_map/all_to_all | solution.py:85
  36.9 40.5 %all-to-all-start.2 = ((bf16[128,32,128]{2,0,1:T(8,128)(2,1)}), bf16[128,32,128]{2,0,1:T(8,128)(2,1)S(1)}, u32[]{:S(2)}, u32[]{:S(2)}) async-start(bf16[128,32,128]{2,0,1:T(8,128)(2,1)} %copy.46), calls=%async_computation.2 | async-start | bytes 2097152 | tf_op jit(solution)/shard_map/all_to_all | solution.py:86
  41.3 183.9 %all-gather.5.cloned.1.call-start = ((), (), s32[]{:S(2)}) async-start(), calls=%async_computation.5 | async-start | bytes 8650752 | tf_op jit(solution)/shard_map/all_gather | solution.py:28
  72.6 1.3 copy-start
  77.4 2.2 copy-start.1
  77.4 3.0 copy-start.2
  124.1 1.6 copy-start.4
  125.0 198.2 %all-gather.7.cloned.1.call-start = ((), (), s32[]{:S(2)}) async-start(), calls=%async_computation.6 | async-start | bytes 8650752 | tf_op jit(solution)/shard_map/all_gather | solution.py:28
  131.6 20.2 %all-to-all-start.3 = ((bf16[8,128,4,128]{3,1,2,0:T(8,128)(2,1)}), bf16[8,128,4,128]{3,1,2,0:T(8,128)(2,1)S(1)}, u32[]{:S(2)}, u32[]{:S(2)}) async-start(bf16[8,128,4,128]{3,1,2,0:T(8,128)(2,1)} %fusion.66), calls=%async_computation.3 | async-start | bytes 2097152 | tf_op jit(solution)/shard_map/all_to_all | solution.py:13
Sparse Core Ops, SparseCore 0:
  125.1 100.0 all-gather.4
  227.8 95.4 all-gather.6
